TPU v7x, 512 devices: a whole 4x8x8 slice. The times are simulated.
512 devices in a mesh: phase: 8 (over x, core), expert: 64 (over y, z).
Axes of the slice: x: 4, y: 8, z: 8, core: 2. Of those that a mesh axis runs over, the one named last changes fastest.
Arguments:
- fwd_acts: bfloat16 [8, 8192, 2048], P('phase', 'expert'), may hold values from -6 to 6
- fwd_routes: int32 [8, 8192, 1], P('phase', 'expert'), may hold values from 0 to 7; in each aligned block of 128 rows (0 to 127, 128 to 255, ..., all dimensions but the last counted through in order) at most 18 rows name the same one
- fwd_weights: float32 [8, 8192, 1], P('phase', 'expert'), may hold values from 0.1 to 1
- fwd_lengths: int32 [8, 16], P('phase'), may hold values from 1 to 2048, 8192 in all within a row
- fwd_tenants: int32 [8, 16], P('phase'), may hold values from 0 to 1
- bwd_acts: bfloat16 [8, 8192, 2048], P('phase', 'expert'), may hold values from -6 to 6
- bwd_routes: int32 [8, 8192, 1], P('phase', 'expert'), may hold values from 0 to 7; in each aligned block of 128 rows (0 to 127, 128 to 255, ..., all dimensions but the last counted through in order) at most 18 rows name the same one
- bwd_weights: float32 [8, 8192, 1], P('phase', 'expert'), may hold values from 0.1 to 1
- bwd_lengths: int32 [8, 16], P('phase'), may hold values from 1 to 2048, 8192 in all within a row
- bwd_tenants: int32 [8, 16], P('phase'), may hold values from 0 to 1
- bwd_cotangent: bfloat16 [8, 8192, 2048], P('phase', 'expert'), may hold values from -6 to 6
- prompts: bfloat16 [8, 2, 10, 2048], P('phase'), may hold values from -6 to 6
- norm_gain: float32 [8, 2048], P('phase'), may hold values from 0.1 to 1.9
- w_gate: bfloat16 [8, 64, 2048, 128], P('phase', 'expert'), may hold values from -0.125 to 0.125
- w_up: bfloat16 [8, 64, 2048, 128], P('phase', 'expert'), may hold values from -0.125 to 0.125
- w_down: bfloat16 [8, 64, 128, 2048], P('phase', 'expert'), may hold values from -0.1875 to 0.1875
Outputs:
- next_acts: bfloat16 [8, 8192, 2048], P('phase', 'expert')
- prev_grads: bfloat16 [8, 8192, 2048], P('phase', 'expert')
- prompt_grads: bfloat16 [8, 2, 10, 2048], P('phase')
Inputs may be any that keep to these rules, and one draw needn't show every extreme that they name: `fwd_routes`: each row names 1 different experts; among the 128 tokens of one device no expert is named by more than 18 rows, a bound that some block reaches. `bwd_routes`: each row names 1 different experts; among the 128 tokens of one device no expert is named by more than 18 rows, a bound that some block reaches.
All inputs are finite; a program needn't handle non-finite values.
Results may differ from a plain program's by a relative error of at most 0.008.
Values may be sent and summed in bfloat16 or wider, within the bound.
No kernel may reach another device: no remote copies, remote signals or barrier semaphores. Data moves between devices by JAX's collectives and lax.ppermute only.
A program may use at most 128 MiB of HBM per device.

v0:
```python
import jax
import jax.numpy as jnp
from jax import lax
from jax.sharding import PartitionSpec as P

EXPERTS = 8
TENANTS = 2
PLEN = 10
CAP = 18
EPS = 1e-06


def shifted(block, axis, distance):
    devices = range(lax.axis_size(axis))
    route = [(i - distance, i) for i in devices if i - distance in devices]
    return lax.ppermute(block, axis, route)


def token_layout(lengths, tenants, tok_count):
    first_row = lax.axis_index("expert") * tok_count
    token_index = first_row + jnp.arange(tok_count, dtype=jnp.int32)
    seg_ends = jnp.cumsum(lengths)
    seg_starts = seg_ends - lengths
    member = (seg_starts[None, :] <= token_index[:, None]).astype(jnp.int32)
    segment = jnp.sum(member, axis=1) - 1
    chosen = (jnp.arange(lengths.shape[0], dtype=jnp.int32)[None, :] == segment[:, None]).astype(
        jnp.int32
    )
    position = token_index - jnp.sum(chosen * seg_starts[None, :], axis=1)
    tenant = jnp.sum(chosen * tenants[None, :], axis=1)
    return (position, tenant)


def prepare(acts, lengths, tenants, prompt_table, gain_row):
    tok_count = acts.shape[0]
    position, tenant = token_layout(lengths, tenants, tok_count)
    prompt_slot = position < PLEN
    flat_index = tenant * PLEN + jnp.minimum(position, PLEN - 1)
    selector = (
        flat_index[:, None] == jnp.arange(TENANTS * PLEN, dtype=jnp.int32)[None, :]
    ) & prompt_slot[:, None]
    flat_table = prompt_table.reshape(TENANTS * PLEN, prompt_table.shape[-1])
    prompt_rows = jnp.dot(
        selector.astype(jnp.bfloat16), flat_table, preferred_element_type=jnp.float32
    ).astype(jnp.bfloat16)
    inputs = jnp.where(prompt_slot[:, None], prompt_rows, acts)
    widened = inputs.astype(jnp.float32)
    inv_scale = lax.rsqrt(jnp.mean(widened * widened, axis=1, keepdims=True) + EPS)
    normed = (widened * inv_scale * gain_row[None, :]).astype(jnp.bfloat16)
    return (selector, widened, inv_scale, normed, prompt_slot)


def routing(routes, weights):
    tok_count, top_count = routes.shape
    flattened = routes.reshape(tok_count * top_count)
    onehot = (flattened[:, None] == jnp.arange(EXPERTS, dtype=jnp.int32)[None, :]).astype(jnp.int32)
    ranking = jnp.sum((jnp.cumsum(onehot, axis=0) - 1) * onehot, axis=1)
    target = (flattened * CAP + ranking).reshape(tok_count, top_count)
    matches = target[:, :, None] == jnp.arange(EXPERTS * CAP, dtype=jnp.int32)[None, None, :]
    picker = jnp.transpose(jnp.any(matches, axis=1).astype(jnp.bfloat16))
    mixing = jnp.sum(jnp.where(matches, weights[:, :, None], 0.0), axis=1)
    return (picker, mixing)


def dispatch(picker, sources):
    shards = lax.axis_size("expert") // EXPERTS
    stacked, tok_count, model_width = sources.shape
    packed = jnp.einsum("qn,mnd->mqd", picker, sources, preferred_element_type=jnp.float32).astype(
        jnp.bfloat16
    )
    packed = jnp.broadcast_to(
        packed.reshape(stacked, 1, EXPERTS * CAP, model_width),
        (stacked, shards, EXPERTS * CAP, model_width),
    )
    packed = packed.reshape(stacked, shards * EXPERTS, CAP, model_width)
    received = lax.all_to_all(packed, "expert", split_axis=1, concat_axis=1, tiled=True)
    return received


def give_back(partial_value):
    shards = lax.axis_size("expert") // EXPERTS
    returned = lax.all_to_all(partial_value, "expert", split_axis=0, concat_axis=0, tiled=True)
    return jnp.sum(
        returned.reshape(shards, EXPERTS * CAP, partial_value.shape[-1]).astype(jnp.float32), axis=0
    )


def expert_forward(slot_rows, gate_weight, up_weight, down_weight):
    gate_pre = jnp.dot(slot_rows, gate_weight, preferred_element_type=jnp.float32)
    upper = jnp.dot(slot_rows, up_weight, preferred_element_type=jnp.float32)
    hidden = (jax.nn.silu(gate_pre) * upper).astype(jnp.bfloat16)
    return jnp.dot(hidden, down_weight, preferred_element_type=jnp.float32).astype(jnp.bfloat16)


def expert_backward(slot_rows, slot_grads, gate_weight, up_weight, down_weight):
    gate_pre = jnp.dot(slot_rows, gate_weight, preferred_element_type=jnp.float32)
    upper = jnp.dot(slot_rows, up_weight, preferred_element_type=jnp.float32)
    contract = (((1,), (1,)), ((), ()))
    hidden_grad = lax.dot_general(
        slot_grads, down_weight, contract, preferred_element_type=jnp.float32
    )
    sigmoid_gate = jax.nn.sigmoid(gate_pre)
    gate_grad = (
        hidden_grad * upper * sigmoid_gate * (1.0 + gate_pre * (1.0 - sigmoid_gate))
    ).astype(jnp.bfloat16)
    up_grad = (hidden_grad * (gate_pre * sigmoid_gate)).astype(jnp.bfloat16)
    back_rows = lax.dot_general(
        gate_grad, gate_weight, contract, preferred_element_type=jnp.float32
    )
    back_rows = back_rows + lax.dot_general(
        up_grad, up_weight, contract, preferred_element_type=jnp.float32
    )
    return back_rows.astype(jnp.bfloat16)


def on_device(
    fwd_acts,
    fwd_routes,
    fwd_weights,
    fwd_lengths,
    fwd_tenants,
    bwd_acts,
    bwd_routes,
    bwd_weights,
    bwd_lengths,
    bwd_tenants,
    bwd_cotangent,
    prompts,
    norm_gain,
    w_gate,
    w_up,
    w_down,
):
    gate_weight = w_gate[0, 0]
    up_weight = w_up[0, 0]
    down_weight = w_down[0, 0]
    gain_row = norm_gain[0]
    prompt_table = prompts[0]
    model_width = fwd_acts.shape[-1]
    fwd_select, fwd_wide, fwd_scale, fwd_normed, fwd_slot = prepare(
        fwd_acts[0], fwd_lengths[0], fwd_tenants[0], prompt_table, gain_row
    )
    fwd_picker, fwd_mixing = routing(fwd_routes[0], fwd_weights[0])
    arrived = dispatch(fwd_picker, fwd_normed[None])
    senders = arrived.shape[1]
    partial_value = expert_forward(
        arrived[0].reshape(senders * CAP, model_width), gate_weight, up_weight, down_weight
    )
    summed = give_back(partial_value.reshape(senders, CAP, model_width))
    mixed_out = fwd_wide + jnp.dot(fwd_mixing, summed, precision=lax.Precision.HIGHEST)
    leaving = mixed_out.astype(jnp.bfloat16)
    next_acts = shifted(leaving, "phase", 1)
    bwd_select, bwd_wide, bwd_scale, bwd_normed, bwd_slot = prepare(
        bwd_acts[0], bwd_lengths[0], bwd_tenants[0], prompt_table, gain_row
    )
    bwd_picker, bwd_mixing = routing(bwd_routes[0], bwd_weights[0])
    cotangent = bwd_cotangent[0]
    arrived_back = dispatch(bwd_picker, jnp.stack([bwd_normed, cotangent]))
    partial_back = expert_backward(
        arrived_back[0].reshape(senders * CAP, model_width),
        arrived_back[1].reshape(senders * CAP, model_width),
        gate_weight,
        up_weight,
        down_weight,
    )
    summed_back = give_back(partial_back.reshape(senders, CAP, model_width))
    normed_grad = jnp.dot(bwd_mixing, summed_back, precision=lax.Precision.HIGHEST)
    scaled = normed_grad * gain_row[None, :]
    inner = jnp.mean(bwd_wide * scaled, axis=1, keepdims=True)
    input_grad = (
        cotangent.astype(jnp.float32) + bwd_scale * scaled - bwd_wide * bwd_scale**3 * inner
    )
    to_prev = jnp.where(bwd_slot[:, None], 0.0, input_grad).astype(jnp.bfloat16)
    prev_grads = shifted(to_prev, "phase", -1)
    local_sums = jnp.dot(
        jnp.transpose(bwd_select.astype(jnp.float32)), input_grad, precision=lax.Precision.HIGHEST
    )
    totals = lax.psum(local_sums, "expert")
    prompt_grads = totals.reshape(1, TENANTS, PLEN, model_width).astype(jnp.bfloat16)
    return (next_acts[None], prev_grads[None], prompt_grads)


def solution(mesh):
    placed = (
        P("phase", "expert", None),
        P("phase", "expert", None),
        P("phase", "expert", None),
        P("phase", None),
        P("phase", None),
        P("phase", "expert", None),
        P("phase", "expert", None),
        P("phase", "expert", None),
        P("phase", None),
        P("phase", None),
        P("phase", "expert", None),
        P("phase", None, None, None),
        P("phase", None),
        P("phase", "expert", None, None),
        P("phase", "expert", None, None),
        P("phase", "expert", None, None),
    )
    return jax.shard_map(
        on_device,
        mesh=mesh,
        in_specs=placed,
        out_specs=(
            P("phase", "expert", None),
            P("phase", "expert", None),
            P("phase", None, None, None),
        ),
        check_vma=False,
    )
```

profile of v0, /device:TPU:36, one launch (start us, length us, event | category | flops | bytes accessed | tf_op | source)
XLA Modules:
  0.0 1311.5 jit_solution(975837895841320012)
XLA Ops:
  0.6 0.0 copy-start
  0.7 0.9 reduce-window_1_clone.1
  1.6 0.7 subtract_bitcast_fusion
  2.2 0.8 reduce-window_clone.1
  3.1 0.7 subtract_bitcast_fusion.1
  3.7 0.9 copy.27
  4.7 0.1 convert_reduce_fusion
  4.8 0.7 select_reduce_fusion.4
  5.5 1.5 multiply_reduce_fusion.2
  7.0 0.7 fusion.49
  7.8 0.2 reduce_window_sum.26
  7.9 0.8 select_reduce_fusion.1
  8.8 0.7 multiply_add_fusion.1
  9.4 1.1 fusion.7
  10.5 2.7 broadcast_in_dim.97
  13.3 7.6 broadcast_in_dim.98
  20.8 16.6 %all-to-all-start = ((bf16[1,64,18,2048]{3,2,0,1:T(8,128)(2,1)}), bf16[1,64,18,2048]{3,2,0,1:T(8,128)(2,1)}, u32[]{:S(2)}, u32[]{:S(2)}) async-start(bf16[1,64,18,2048]{3,2,0,1:T(8,128)(2,1)} %bitcast.72), calls=%async_computation | async-start | bytes 12582912 | tf_op jit(solution)/shard_map/all_to_all | solution.py:76
  37.5 0.1 fusion.48
  37.6 0.2 reduce_window_sum.27
  37.8 0.0 copy-done.10
  37.8 0.1 select_reduce_fusion.2
  37.8 0.2 select_reduce_fusion
  38.0 1.5 multiply_reduce_fusion.1
  39.6 0.2 fusion.25
  39.7 0.5 fusion.3
  40.2 2.3 copy.29
  42.5 214.9 %all-to-all-done = bf16[1,64,18,2048]{3,2,0,1:T(8,128)(2,1)} async-done(((bf16[1,64,18,2048]{3,2,0,1:T(8,128)(2,1)}), bf16[1,64,18,2048]{3,2,0,1:T(8,128)(2,1)}, u32[]{:S(2)}, u32[]{:S(2)}) %all-to-all-start) | async-done | bytes 4718624 | tf_op jit(solution)/shard_map/all_to_all | solution.py:76
  257.4 8.3 broadcast_in_dim.104
  265.7 20.2 %all-to-all-start.2 = ((bf16[2,64,18,2048]{3,0,2,1:T(2,128)(2,1)}), bf16[2,64,18,2048]{3,0,2,1:T(2,128)(2,1)}, u32[]{:S(2)}, u32[]{:S(2)}) async-start(bf16[2,64,18,2048]{3,0,2,1:T(2,128)(2,1)} %bitcast.71), calls=%async_computation.2 | async-start | bytes 18874368 | tf_op jit(solution)/shard_map/all_to_all | solution.py:76
  285.9 0.0 copy-start.2
  285.9 7.8 reshape_squeeze.21
  293.8 4.6 fusion.37
  298.3 9.6 convolution_convert_fusion
  307.9 7.6 reshape.228
  315.5 246.5 %all-to-all-done.2 = bf16[2,64,18,2048]{3,0,2,1:T(2,128)(2,1)} async-done(((bf16[2,64,18,2048]{3,0,2,1:T(2,128)(2,1)}), bf16[2,64,18,2048]{3,0,2,1:T(2,128)(2,1)}, u32[]{:S(2)}, u32[]{:S(2)}) %all-to-all-start.2) | async-done | bytes 9437216 | tf_op jit(solution)/shard_map/all_to_all | solution.py:76
  562.0 44.8 %all-to-all-start.1 = ((bf16[64,18,2048]{2,1,0:T(8,128)(2,1)}), bf16[64,18,2048]{2,1,0:T(8,128)(2,1)}, u32[]{:S(2)}, u32[]{:S(2)}) async-start(bf16[64,18,2048]{2,1,0:T(8,128)(2,1)} %reshape.228), calls=%async_computation.1 | async-start | bytes 12582912 | tf_op jit(solution)/shard_map/all_to_all | solution.py:82
  606.8 48.0 %slice_reduce_fusion = (bf16[64,18,2048]{2,1,0:T(8,128)(2,1)}, bf16[64,18,2048]{2,1,0:T(8,128)(2,1)}) fusion(bf16[2,64,18,2048]{3,0,2,1:T(2,128)(2,1)} %all-to-all-done.2), kind=kLoop, calls=%fused_computation.1 | loop fusion | bytes 18874368 | tf_op jit(solution)/shard_map/slice | solution.py:160
  654.8 7.7 reshape_squeeze.23
  662.6 7.7 reshape_squeeze.24
  670.3 4.0 fusion.26
  674.3 0.0 copy-done.3
  674.3 2.2 fusion.35
  676.5 11.1 fusion.12
  687.6 7.5 fusion
  695.2 7.6 reshape.230
  702.8 99.0 %all-to-all-done.1 = bf16[64,18,2048]{2,1,0:T(8,128)(2,1)} async-done(((bf16[64,18,2048]{2,1,0:T(8,128)(2,1)}), bf16[64,18,2048]{2,1,0:T(8,128)(2,1)}, u32[]{:S(2)}, u32[]{:S(2)}) %all-to-all-start.1) | async-done | bytes 4718624 | tf_op jit(solution)/shard_map/all_to_all | solution.py:82
  801.8 16.9 %all-to-all-start.3 = ((bf16[64,18,2048]{2,1,0:T(8,128)(2,1)}), bf16[64,18,2048]{2,1,0:T(8,128)(2,1)}, u32[]{:S(2)}, u32[]{:S(2)}) async-start(bf16[64,18,2048]{2,1,0:T(8,128)(2,1)} %reshape.230), calls=%async_computation.3 | async-start | bytes 12582912 | tf_op jit(solution)/shard_map/all_to_all | solution.py:82
  818.7 8.5 reshape.231
  827.3 5.8 reduce_sum.130
  833.0 3.1 fusion.4
  836.2 1.9 collective-permute-start
  838.1 175.9 %all-to-all-done.3 = bf16[64,18,2048]{2,1,0:T(8,128)(2,1)} async-done(((bf16[64,18,2048]{2,1,0:T(8,128)(2,1)}), bf16[64,18,2048]{2,1,0:T(8,128)(2,1)}, u32[]{:S(2)}, u32[]{:S(2)}) %all-to-all-start.3) | async-done | bytes 4718624 | tf_op jit(solution)/shard_map/all_to_all | solution.py:82
  1014.0 8.6 reshape.233
  1022.5 4.7 reduce_sum.136
  1027.3 1.2 multiply_reduce_fusion
  1028.5 0.4 select_convert_fusion
  1028.9 1.9 collective-permute-start.1
  1030.8 0.0 collective-permute-done
  1030.8 0.5 fusion.53
  1031.3 276.7 %all-reduce.1 = bf16[20,2048]{1,0:T(8,128)(2,1)S(1)} all-reduce(f32[20,2048]{1,0:T(8,128)S(1)} %fusion.53), channel_id=1, replica_groups=mesh['phase'=8,'expert'=64] {'expert'}, use_global_device_ids=true, to_apply=%region_17.18 | all-reduce | flops 40960 | bytes 245760 | tf_op jit(solution)/shard_map/psum | solution.py:178
  1308.1 0.7 copy.30
  1308.8 0.0 collective-permute-done.1
  1308.8 1.9 copy.37
  1310.7 0.8 copy.38
  (30 shorter events, 0.2 us)
Async XLA Ops:
  0.6 297.7 %copy-start = (bf16[1,1,2048,128]{3,2,1,0:T(8,128)(2,1)S(1)}, bf16[1,1,2048,128]{3,2,1,0:T(8,128)(2,1)}, u32[]{:S(2)}) copy-start(bf16[1,1,2048,128]{3,2,1,0:T(8,128)(2,1)} %param.30) | copy-start | bytes 1572868
  20.8 16.7 %copy-start.7 = (s32[1,128,1]{1,2,0:T(1,128)S(1)}, s32[1,128,1]{1,2,0:T(1,128)}, u32[]{:S(2)}) copy-start(s32[1,128,1]{1,2,0:T(1,128)} %param.22) | copy-start | bytes 1540
  20.8 16.9 %copy-start.10 = (s32[1,16]{1,0:T(1,128)S(1)}, s32[1,16]{1,0:T(1,128)}, u32[]{:S(2)}) copy-start(s32[1,16]{1,0:T(1,128)} %param.25) | copy-start | bytes 196
  20.8 18.7 %copy-start.6 = (f32[1,2048]{1,0:T(1,128)S(1)}, f32[1,2048]{1,0:T(1,128)}, u32[]{:S(2)}) copy-start(f32[1,2048]{1,0:T(1,128)} %param.28) | copy-start | bytes 24580
  20.8 18.9 %copy-start.4 = (bf16[1,128,2048]{2,1,0:T(8,128)(2,1)S(1)}, bf16[1,128,2048]{2,1,0:T(8,128)(2,1)}, u32[]{:S(2)}) copy-start(bf16[1,128,2048]{2,1,0:T(8,128)(2,1)} %param.26) | copy-start | bytes 1572868
  20.8 236.6 %all-to-all-start = ((bf16[1,64,18,2048]{3,2,0,1:T(8,128)(2,1)}), bf16[1,64,18,2048]{3,2,0,1:T(8,128)(2,1)}, u32[]{:S(2)}, u32[]{:S(2)}) async-start(bf16[1,64,18,2048]{3,2,0,1:T(8,128)(2,1)} %bitcast.72), calls=%async_computation | async-start | bytes 12582912 | tf_op jit(solution)/shard_map/all_to_all | solution.py:76
  265.7 296.3 %all-to-all-start.2 = ((bf16[2,64,18,2048]{3,0,2,1:T(2,128)(2,1)}), bf16[2,64,18,2048]{3,0,2,1:T(2,128)(2,1)}, u32[]{:S(2)}, u32[]{:S(2)}) async-start(bf16[2,64,18,2048]{3,0,2,1:T(2,128)(2,1)} %bitcast.71), calls=%async_computation.2 | async-start | bytes 18874368 | tf_op jit(solution)/shard_map/all_to_all | solution.py:76
  285.9 7.8 copy-start.2
  562.0 239.8 %all-to-all-start.1 = ((bf16[64,18,2048]{2,1,0:T(8,128)(2,1)}), bf16[64,18,2048]{2,1,0:T(8,128)(2,1)}, u32[]{:S(2)}, u32[]{:S(2)}) async-start(bf16[64,18,2048]{2,1,0:T(8,128)(2,1)} %reshape.228), calls=%async_computation.1 | async-start | bytes 12582912 | tf_op jit(solution)/shard_map/all_to_all | solution.py:82
  670.2 4.0 copy-start.1
  670.3 4.0 copy-start.3
  801.8 212.2 %all-to-all-start.3 = ((bf16[64,18,2048]{2,1,0:T(8,128)(2,1)}), bf16[64,18,2048]{2,1,0:T(8,128)(2,1)}, u32[]{:S(2)}, u32[]{:S(2)}) async-start(bf16[64,18,2048]{2,1,0:T(8,128)(2,1)} %reshape.230), calls=%async_computation.3 | async-start | bytes 12582912 | tf_op jit(solution)/shard_map/all_to_all | solution.py:82
  827.3 5.8 copy-start.8
  836.2 194.6 %collective-permute-start = (bf16[128,2048]{1,0:T(8,128)(2,1)}, bf16[128,2048]{1,0:T(8,128)(2,1)}, u32[]{:S(2)}, u32[]{:S(2)}) collective-permute-start(bf16[128,2048]{1,0:T(8,128)(2,1)} %fusion.4), channel_id=1, source_target_pairs={{0,64},{64,128},{128,192},{192,256},{256,320},{320,384},{384,448},... | collective-permute-start | bytes 1572872 | tf_op jit(solution)/shard_map/ppermute | solution.py:16
  1022.5 4.7 copy-start.9
  1022.5 6.0 copy-start.5
  1028.9 279.9 %collective-permute-start.1 = (bf16[128,2048]{1,0:T(8,128)(2,1)S(1)}, bf16[128,2048]{1,0:T(8,128)(2,1)S(1)}, u32[]{:S(2)}, u32[]{:S(2)}) collective-permute-start(bf16[128,2048]{1,0:T(8,128)(2,1)S(1)} %get-tuple-element.23), channel_id=1, source_target_pairs={{64,0},{128,64},{192,128},{256,192},{320,256},{384,320},{448,384},... | collective-permute-start | bytes 1572872 | tf_op jit(solution)/shard_map/ppermute | solution.py:16
where the time goes:
time: 1310 us
  waiting for transfers between devices  736 us (56%)
  blocking collectives  277 us (21%)
  local copies, waits for them, and re-layouts  129 us (10%)
  starting transfers between devices  102 us (8%)
  matrix products  48.4 us (4%)
  other arithmetic  17.9 us (1%)
    all_to_all x2, waiting for transfers between devices, dispatch(): lax.all_to_all(packed, 'expert', split_axis=1, concat_axis=1, tiled=True)  461 us
    psum x1, blocking collectives, on_device(): totals = lax.psum(local_sums, 'expert')  277 us
    all_to_all x2, waiting for transfers between devices, give_back(): lax.all_to_all(partial_value, 'expert', split_axis=0, concat_axis=0, tile...  275 us
    all_to_all x2, starting transfers between devices, give_back(): lax.all_to_all(partial_value, 'expert', split_axis=0, concat_axis=0, tile...  61.7 us
    slice x1, local copies, waits for them, and re-layouts, on_device(): arrived_back[0].reshape(senders * CAP, model_width)  48 us
    all_to_all x2, starting transfers between devices, dispatch(): lax.all_to_all(packed, 'expert', split_axis=1, concat_axis=1, tiled=True)  36.9 us
  transfers between devices with their start and end apart: 6, of which 4 were waited for; matrix products, arithmetic and copies ran while one was open for 13% of the time, Pallas kernels for 0%

commit v1 on v0

--- a/solution.py
+++ b/solution.py
@@ -175,7 +175,7 @@
     local_sums = jnp.dot(
         jnp.transpose(bwd_select.astype(jnp.float32)), input_grad, precision=lax.Precision.HIGHEST
     )
-    totals = lax.psum(local_sums, "expert")
+    totals = jnp.sum(lax.all_gather(local_sums, "expert"), axis=0)
     prompt_grads = totals.reshape(1, TENANTS, PLEN, model_width).astype(jnp.bfloat16)
     return (next_acts[None], prev_grads[None], prompt_grads)
 

time: 1310 us -> 1070 us (0.82)
  the two profiles are of different devices: /device:TPU:36 before, /device:TPU:27 now
where the time goes in v1:
time: 1070 us
  blocking collectives  619 us (58%)
  waiting for transfers between devices  201 us (19%)
  local copies, waits for them, and re-layouts  130 us (12%)
  matrix products  47.5 us (4%)
  starting transfers between devices  28.1 us (3%)
  other arithmetic  26.8 us (3%)
  between operations  14.3 us (1%)
    all_to_all x2, blocking collectives, dispatch(): lax.all_to_all(packed, 'expert', split_axis=1, concat_axis=1, tiled=True)  433 us
    all_to_all x1, waiting for transfers between devices, give_back(): lax.all_to_all(partial_value, 'expert', split_axis=0, concat_axis=0, tile...  192 us
    all_to_all x1, blocking collectives, give_back(): lax.all_to_all(partial_value, 'expert', split_axis=0, concat_axis=0, tile...  186 us
    slice x1, local copies, waits for them, and re-layouts, on_device(): arrived_back[0].reshape(senders * CAP, model_width)  52.7 us
  transfers between devices with their start and end apart: 4, of which 3 were waited for; matrix products, arithmetic and copies ran while one was open for 5% of the time, Pallas kernels for 0%

profile of v1, /device:TPU:27, one launch (start us, length us, event | category | flops | bytes accessed | tf_op | source)
XLA Modules:
  0.0 1065.8 jit_solution(1057188118395878668)
XLA Ops:
  7.2 0.0 copy-start
  7.2 0.9 reduce-window_1_clone.1
  8.1 0.7 subtract_bitcast_fusion
  8.7 0.8 reduce-window_clone.1
  9.6 0.7 subtract_bitcast_fusion.1
  10.2 0.1 convert_reduce_fusion
  10.3 0.7 select_reduce_fusion.2
  11.1 0.9 copy.26
  12.1 1.5 multiply_reduce_fusion.1
  13.6 0.7 fusion.48
  14.3 0.2 reduce_window_sum.27
  14.5 0.8 select_reduce_fusion
  15.3 0.7 multiply_add_fusion
  16.0 0.8 fusion.25
  16.8 1.5 fusion.3
  18.3 1.2 copy.28
  19.6 6.3 broadcast_in_dim.104
  25.9 267.1 %all_to_all.20 = bf16[2,64,18,2048]{3,0,2,1:T(2,128)(2,1)S(1)} all-to-all(bf16[2,64,18,2048]{3,0,2,1:T(2,128)(2,1)S(1)} %bitcast.73), channel_id=1, replica_groups=mesh['phase'=8,'expert'=64] {'expert'}, dimensions={1} | all-to-all | bytes 18874368 | tf_op jit(solution)/shard_map/all_to_all | solution.py:76
  293.0 52.7 %slice_reduce_fusion = (bf16[64,18,2048]{2,1,0:T(8,128)(2,1)}, bf16[64,18,2048]{2,1,0:T(8,128)(2,1)}) fusion(bf16[2,64,18,2048]{3,0,2,1:T(2,128)(2,1)S(1)} %all_to_all.20), kind=kLoop, calls=%fused_computation.1 | loop fusion | bytes 18874368 | tf_op jit(solution)/shard_map/slice | solution.py:160
  345.7 7.7 reshape_squeeze.23
  353.4 7.8 reshape_squeeze.24
  361.2 3.9 fusion.26
  365.1 0.0 copy-done.1
  365.1 0.0 copy-done.2
  365.1 1.4 fusion.35
  366.5 0.0 copy-done
  366.5 10.8 %fusion.12 = f32[1152,2048]{1,0:T(8,128)} fusion(f32[1152,128]{1,0:T(8,128)S(1)} %fusion.26, bf16[1152,2048]{1,0:T(8,128)(2,1)} %reshape_squeeze.24, f32[1152,128]{1,0:T(8,128)S(1)} %fusion.35, bf16[1,1,2048,128]{3,2,1,0:T(8,128)(2,1)S(1)} %copy-done, bf16[1,1,2048,128]{3,2,1,0:T(8,128)(2,1)S(1)} %copy-done.2), kind=kOutput, calls=%fused_computation.25 | convolution fusion | flops 1209434112 | bytes 16384000 | tf_op jit(solution)/shard_map/dot_general | solution.py:107
  377.4 7.3 fusion
  384.7 7.6 reshape.230
  392.2 9.6 all-to-all-start.3
  401.9 0.0 all-gather.4.cloned.1.call-start
  402.0 0.1 fusion.49
  402.0 0.2 reduce_window_sum.26
  402.2 0.1 select_reduce_fusion.4
  402.3 0.2 select_reduce_fusion.1
  402.5 1.5 multiply_reduce_fusion.2
  404.0 192.0 %all-to-all-done.3 = bf16[64,18,2048]{2,1,0:T(8,128)(2,1)} async-done(((bf16[64,18,2048]{2,1,0:T(8,128)(2,1)}), bf16[64,18,2048]{2,1,0:T(8,128)(2,1)}, u32[]{:S(2)}, u32[]{:S(2)}) %all-to-all-start.3) | async-done | bytes 4718624 | tf_op jit(solution)/shard_map/all_to_all | solution.py:82
  596.0 8.6 reshape.233
  604.7 5.7 reduce_sum.145
  610.3 0.0 copy-done.5
  610.3 2.5 multiply_reduce_fusion
  612.8 2.2 select_convert_fusion
  615.0 1.2 convolution_bitcast_fusion
  616.2 0.0 all-gather.4.cloned.1.call-update
  616.2 0.4 fusion.7
  616.6 2.8 broadcast_in_dim.97
  619.4 7.6 broadcast_in_dim.98
  627.0 165.6 %all_to_all.21 = bf16[1,64,18,2048]{3,2,0,1:T(8,128)(2,1)} all-to-all(bf16[1,64,18,2048]{3,2,0,1:T(8,128)(2,1)} %bitcast.74), channel_id=1, replica_groups=mesh['phase'=8,'expert'=64] {'expert'}, dimensions={1} | all-to-all | bytes 9437184 | tf_op jit(solution)/shard_map/all_to_all | solution.py:76
  792.6 7.7 reshape_squeeze.21
  800.3 3.7 fusion.37
  804.0 9.5 convolution_convert_fusion
  813.5 7.6 reshape.228
  821.1 186.3 %all_to_all.22 = bf16[64,18,2048]{2,1,0:T(8,128)(2,1)} all-to-all(bf16[64,18,2048]{2,1,0:T(8,128)(2,1)} %reshape.228), channel_id=1, replica_groups=mesh['phase'=8,'expert'=64] {'expert'}, dimensions={0} | all-to-all | bytes 9437184 | tf_op jit(solution)/shard_map/all_to_all | solution.py:82
  1007.4 8.6 reshape.231
  1016.0 5.8 reduce_sum.139
  1021.8 2.4 fusion.4
  1024.2 16.5 %collective-permute-start = (bf16[128,2048]{1,0:T(8,128)(2,1)S(1)}, bf16[128,2048]{1,0:T(8,128)(2,1)S(1)}, u32[]{:S(2)}, u32[]{:S(2)}) collective-permute-start(bf16[128,2048]{1,0:T(8,128)(2,1)S(1)} %fusion.4), channel_id=1, source_target_pairs={{0,64},{64,128},{128,192},{192,256},{256,320},{320,384},{384,448},... | collective-permute-start | bytes 1572872 | tf_op jit(solution)/shard_map/ppermute | solution.py:16
  1040.7 1.9 collective-permute-start.1
  1042.6 4.2 collective-permute-done
  1046.8 4.4 collective-permute-done.1
  1051.2 5.4 reduce_sum.147
  1056.7 0.7 copy.29
  1057.4 0.8 copy.34
  1058.2 0.8 copy.35
  (28 shorter events, 0.2 us)
Async XLA Ops:
  7.2 359.4 %copy-start = (bf16[1,1,2048,128]{3,2,1,0:T(8,128)(2,1)S(1)}, bf16[1,1,2048,128]{3,2,1,0:T(8,128)(2,1)}, u32[]{:S(2)}) copy-start(bf16[1,1,2048,128]{3,2,1,0:T(8,128)(2,1)} %param.30) | copy-start | bytes 1572868
  353.4 7.8 copy-start.3
  361.2 3.9 copy-start.1
  361.2 3.9 copy-start.2
  392.2 9.7 copy-start.6
  392.2 10.0 copy-start.9
  392.2 203.8 %all-to-all-start.3 = ((bf16[64,18,2048]{2,1,0:T(8,128)(2,1)}), bf16[64,18,2048]{2,1,0:T(8,128)(2,1)}, u32[]{:S(2)}, u32[]{:S(2)}) async-start(bf16[64,18,2048]{2,1,0:T(8,128)(2,1)} %reshape.230), calls=%async_computation.3 | async-start | bytes 12582912 | tf_op jit(solution)/shard_map/all_to_all | solution.py:82
  401.9 649.3 %all-gather.4.cloned.1.call-start = ((), (), s32[]{:S(2)}) async-start(), calls=%async_computation.4 | async-start | bytes 12779520 | tf_op jit(solution)/shard_map/all_gather | solution.py:178
  604.6 5.7 copy-start.5
  604.6 5.7 copy-start.7
  1016.0 5.8 copy-start.8
  1016.0 24.7 %copy-start.4 = (bf16[128,2048]{1,0:T(8,128)(2,1)S(1)}, bf16[128,2048]{1,0:T(8,128)(2,1)}, u32[]{:S(2)}) copy-start(bf16[128,2048]{1,0:T(8,128)(2,1)} %get-tuple-element.20) | copy-start | bytes 1572868
  1024.2 22.6 %collective-permute-start = (bf16[128,2048]{1,0:T(8,128)(2,1)S(1)}, bf16[128,2048]{1,0:T(8,128)(2,1)S(1)}, u32[]{:S(2)}, u32[]{:S(2)}) collective-permute-start(bf16[128,2048]{1,0:T(8,128)(2,1)S(1)} %fusion.4), channel_id=1, source_target_pairs={{0,64},{64,128},{128,192},{192,256},{256,320},{320,384},{384,448},... | collective-permute-start | bytes 1572872 | tf_op jit(solution)/shard_map/ppermute | solution.py:16
  1040.7 10.5 collective-permute-start.1
Sparse Core Ops, SparseCore 0:
  616.4 406.5 all-gather.3
